TPU v7x, 32 devices: a whole 2x2x4 slice. The times are simulated.
32 devices in a mesh: tower: 4 (over y, x), rank: 8 (over z, core).
Axes of the slice: x: 2, y: 2, z: 4, core: 2. Of those that a mesh axis runs over, the one named last changes fastest.
Arguments:
- pooled: bfloat16 [2, 2048, 1024], P(None, ('tower', 'rank')), may hold values from -8 to 8
- feature_order: int32 [4, 4], P('tower'), may hold values from 0 to 3, as said below
- cross_weight: bfloat16 [4, 3, 512, 512], P('tower'), may hold values from -0.25 to 0.25
- cross_bias: float32 [4, 3, 512], P('tower'), may hold values from -3 to 3
- compress_weight: bfloat16 [4, 128, 512], P('tower'), may hold values from -0.25 to 0.25
- norm_gain: float32 [4, 128], P('tower'), may hold values from 0.1 to 1.9
- mlp_weight: bfloat16 [4096, 512], P(('tower', 'rank')), may hold values from -0.25 to 0.25
- mlp_bias: bfloat16 [4096], P(('tower', 'rank')), may hold values from -3 to 3
- out_weight: bfloat16 [4096], P(('tower', 'rank')), may hold values from -0.09375 to 0.09375
Outputs:
- logits: float32 [2, 8, 128], P(None, 'rank', 'tower')
Inputs may be any that keep to these rules, and one draw needn't show every extreme that they name: `feature_order`: each row is an ordering of 0 to 3.
All inputs are finite; a program needn't handle non-finite values.
Results may differ from a plain program's by a relative error of at most 0.0076.
Values may be sent and summed in bfloat16 or wider, within the bound.
A program may use at most 64 MiB of HBM per device.

v0:
```python
import jax
import jax.numpy as jnp
from jax import lax
from jax.sharding import PartitionSpec as P

E = 128
CD = 128


epsilon = 1e-06


def tower_block(first, weights, biases, compress, gain):
    first_f = first.astype(jnp.float32)
    current = first
    for layer in range(weights.shape[0]):
        product = (
            jnp.dot(weights[layer], current, preferred_element_type=jnp.float32)
            + biases[layer][:, None]
        )
        current = (first_f * product + current.astype(jnp.float32)).astype(jnp.bfloat16)
    squeezed = jnp.dot(compress, current, preferred_element_type=jnp.float32)
    inverse_rms = lax.rsqrt(jnp.mean(squeezed * squeezed, axis=0, keepdims=True) + epsilon)
    return (squeezed * inverse_rms * gain[:, None]).astype(jnp.bfloat16)


def interact(joined):
    samples_now = joined.shape[1]
    values_f = joined.astype(jnp.float32).reshape(-1, CD, samples_now)
    gram = jnp.einsum("tck,uck->tuk", values_f, values_f, precision=lax.Precision.HIGHEST) / CD
    mixed = values_f + jnp.einsum("tuk,uck->tck", gram, values_f, precision=lax.Precision.HIGHEST)
    return mixed.reshape(-1, samples_now).astype(jnp.bfloat16)


def logit_terms(hidden_rows, hidden_bias, hidden_out, features):
    hidden = (
        jnp.dot(hidden_rows, features, preferred_element_type=jnp.float32)
        + hidden_bias.astype(jnp.float32)[:, None]
    )
    return jnp.sum(
        jax.nn.relu(hidden) * hidden_out.astype(jnp.float32)[:, None], axis=0, keepdims=True
    )


def on_device(
    pooled,
    feature_order,
    cross_weight,
    cross_bias,
    compress_weight,
    norm_gain,
    mlp_weight,
    mlp_bias,
    out_weight,
):
    micro_count = pooled.shape[0]
    arriving = [
        lax.all_to_all(pooled[batch], "rank", split_axis=1, concat_axis=0, tiled=True)
        for batch in range(micro_count)
    ]
    hidden_rows, hidden_bias, hidden_out = (
        lax.all_gather(mlp_weight, "rank", axis=0, tiled=True),
        lax.all_gather(mlp_bias, "rank", axis=0, tiled=True),
        lax.all_gather(out_weight, "rank", axis=0, tiled=True),
    )
    results = []
    for batch in range(micro_count):
        arrived = arriving[batch]
        samples_here = arrived.shape[1]
        first = jnp.take(arrived.reshape(-1, E, samples_here), feature_order[0], axis=0).reshape(
            -1, samples_here
        )
        compressed = tower_block(
            first, cross_weight[0], cross_bias[0], compress_weight[0], norm_gain[0]
        )
        all_towers = lax.all_gather(compressed, "tower", axis=0, tiled=True)
        partial_value = logit_terms(hidden_rows, hidden_bias, hidden_out, interact(all_towers))
        logit_row = lax.psum_scatter(partial_value, "tower", scatter_dimension=1, tiled=True)
        results.append(logit_row)
    return jnp.stack(results)


def solution(mesh):
    return jax.shard_map(
        on_device,
        mesh=mesh,
        in_specs=(
            P(None, ("tower", "rank"), None),
            P("tower", None),
            P("tower", None, None, None),
            P("tower", None, None),
            P("tower", None, None),
            P("tower", None),
            P(("tower", "rank"), None),
            P(("tower", "rank")),
            P(("tower", "rank")),
        ),
        out_specs=P(None, "rank", "tower"),
        check_vma=False,
    )
```

profile of v0, /device:TPU:0, one launch (start us, length us, event | category | flops | bytes accessed | tf_op | source)
XLA Modules:
  0.0 129.5 jit_solution(2807232870646016834)
XLA Ops:
  6.5 0.0 copy-start
  6.5 0.0 copy-start.7
  6.5 0.0 copy-start.3
  6.5 0.0 copy-start.4
  6.5 0.0 copy-start.1
  6.5 1.0 slice_bitcast_fusion.1
  7.6 0.0 copy-start.5
  7.6 0.7 copy.34
  8.3 6.4 %all-to-all-start = ((bf16[64,8,128]{2,0,1:T(8,128)(2,1)}), bf16[64,8,128]{2,0,1:T(8,128)(2,1)S(1)}, u32[]{:S(2)}, u32[]{:S(2)}) async-start(bf16[64,8,128]{2,0,1:T(8,128)(2,1)} %copy.34), calls=%async_computation | async-start | bytes 262144 | tf_op jit(solution)/shard_map/all_to_all | solution.py:58
  14.6 0.0 all-gather.4.cloned.1.call-start
  14.7 0.7 all-gather.4.cloned.1.call-update
  15.4 0.7 compare_select_fusion
  16.1 0.7 copy.41
  16.8 0.0 copy-done.7
  16.8 4.6 %all-to-all-done = bf16[64,8,128]{2,0,1:T(8,128)(2,1)S(1)} async-done(((bf16[64,8,128]{2,0,1:T(8,128)(2,1)}), bf16[64,8,128]{2,0,1:T(8,128)(2,1)S(1)}, u32[]{:S(2)}, u32[]{:S(2)}) %all-to-all-start) | async-done | bytes 131104 | tf_op jit(solution)/shard_map/all_to_all | solution.py:58
  21.4 3.4 %all-to-all-start.1 = ((bf16[64,8,128]{2,0,1:T(8,128)(2,1)}), bf16[64,8,128]{2,0,1:T(8,128)(2,1)S(1)}, u32[]{:S(2)}, u32[]{:S(2)}) async-start(bf16[64,8,128]{2,0,1:T(8,128)(2,1)} %copy.41), calls=%async_computation.1 | async-start | bytes 262144 | tf_op jit(solution)/shard_map/all_to_all | solution.py:58
  24.8 0.0 reduce-scatter.7.cloned.1.call-start
  24.8 0.0 copy-done.3
  24.8 12.2 %all-gather = bf16[8,1,128]{2,1,0:T(2,128)(2,1)S(1)} all-gather(bf16[1,1,128]{2,1,0:T(2,128)(2,1)S(1)} %bitcast.203), channel_id=1, replica_groups=mesh['tower'=4,'rank'=8] {'rank'}, dimensions={0}, use_global_device_ids=true | all-gather | bytes 2304 | tf_op jit(solution)/shard_map/all_gather | solution.py:63
  37.1 0.0 copy-done.4
  37.1 10.3 %all-gather.1 = bf16[8,1,128]{2,1,0:T(2,128)(2,1)S(1)} all-gather(bf16[1,1,128]{2,1,0:T(2,128)(2,1)S(1)} %bitcast.204), channel_id=1, replica_groups=mesh['tower'=4,'rank'=8] {'rank'}, dimensions={0}, use_global_device_ids=true | all-gather | bytes 2304 | tf_op jit(solution)/shard_map/all_gather | solution.py:64
  47.4 0.0 copy-done.1
  47.4 0.6 gather_fusion
  48.0 0.0 all-to-all-done.1
  48.0 0.6 gather_fusion.1
  48.6 0.1 broadcast_select_fusion.1
  48.7 0.1 copy.51
  48.8 0.1 copy.50
  49.0 0.0 copy-done.5
  49.0 0.3 fusion.30
  49.3 0.3 fusion.31
  49.6 0.3 fusion.34
  49.9 0.0 copy-done
  50.0 0.0 copy-start.2
  50.0 0.5 multiply_reduce_fusion
  50.5 0.3 fusion.32
  50.8 0.5 multiply_reduce_fusion.1
  51.3 0.0 copy-done.2
  51.3 0.1 fusion.66
  51.4 8.5 %all_gather.15 = bf16[512,128]{1,0:T(8,128)(2,1)S(1)} all-gather(bf16[128,128]{1,0:T(8,128)(2,1)S(1)} %get-tuple-element.11), channel_id=1, replica_groups=mesh['tower'=4,'rank'=8] {'tower'}, dimensions={0}, use_global_device_ids=true | all-gather | bytes 163840 | tf_op jit(solution)/shard_map/all_gather | solution.py:76
  59.9 0.1 copy.36
  60.0 8.5 %all_gather.19 = bf16[512,128]{1,0:T(8,128)(2,1)S(1)} all-gather(bf16[128,128]{1,0:T(8,128)(2,1)S(1)} %get-tuple-element.12), channel_id=1, replica_groups=mesh['tower'=4,'rank'=8] {'tower'}, dimensions={0}, use_global_device_ids=true | all-gather | bytes 163840 | tf_op jit(solution)/shard_map/all_gather | solution.py:76
  68.5 0.1 copy.43
  68.6 0.3 fusion.12
  68.9 0.3 fusion.7
  69.2 0.7 fusion.28
  69.9 0.7 fusion.29
  70.6 0.0 all-gather.4.cloned.1.call-done
  70.6 0.0 copy-start.6
  70.6 1.9 %fusion.5 = f32[128]{0:T(128)S(1)} fusion(bf16[1024,512]{1,0:T(8,128)(2,1)} %all-gather.4.cloned.1.call-done, f32[1024]{0:T(1024)S(1)} %bitcast.190, f32[1024]{0:T(1024)S(1)} %bitcast.188, bf16[16,8,4,128]{3,2,1,0:T(4,128)(2,1)S(1)} %bitcast.185), kind=kOutput, calls=%fused_computation.9 | convolution fusion | flops 134741888 | bytes 1188352 | tf_op jit(solution)/shard_map/dot_general | solution.py:37
  72.5 0.8 copy.52
  73.2 0.0 reduce-scatter.7.cloned.1.call-update
  73.3 0.0 reduce-scatter.9.cloned.1.call-start
  73.3 0.0 copy-done.6
  73.3 0.6 fusion.4
  73.9 0.7 copy.54
  74.6 0.0 reduce-scatter.9.cloned.1.call-update
  74.7 20.1 %reduce-scatter.7.cloned.1.call-done = f32[32,1]{1,0:T(8,128)} async-done(((f32[128,1]{1,0:T(8,128)}), f32[32,1]{1,0:T(8,128)}) %reduce-scatter.7.cloned.1.call-update) | async-done | bytes 144
  94.7 0.8 copy.53
  95.5 26.0 %reduce-scatter.9.cloned.1.call-done = f32[32,1]{1,0:T(8,128)} async-done(((f32[128,1]{1,0:T(8,128)}), f32[32,1]{1,0:T(8,128)}) %reduce-scatter.9.cloned.1.call-update) | async-done | bytes 144
  121.6 0.8 copy.55
  122.4 0.6 pad_maximum_fusion
  (8 shorter events, 0.1 us)
Async XLA Ops:
  6.5 43.4 %copy-start = (bf16[1,128,512]{2,1,0:T(8,128)(2,1)S(1)}, bf16[1,128,512]{2,1,0:T(8,128)(2,1)}, u32[]{:S(2)}) copy-start(bf16[1,128,512]{2,1,0:T(8,128)(2,1)} %param.15) | copy-start | bytes 393220
  6.5 10.2 %copy-start.7 = (s32[1,4]{1,0:T(1,128)S(1)}, s32[1,4]{1,0:T(1,128)}, u32[]{:S(2)}) copy-start(s32[1,4]{1,0:T(1,128)} %param.12) | copy-start | bytes 52
  6.5 18.3 %copy-start.3 = (bf16[128]{0:T(256)(128)(2,1)S(1)}, bf16[128]{0:T(256)(128)(2,1)}, u32[]{:S(2)}) copy-start(bf16[128]{0:T(256)(128)(2,1)} %param.18) | copy-start | bytes 772
  6.5 30.5 %copy-start.4 = (bf16[128]{0:T(256)(128)(2,1)S(1)}, bf16[128]{0:T(256)(128)(2,1)}, u32[]{:S(2)}) copy-start(bf16[128]{0:T(256)(128)(2,1)} %param.19) | copy-start | bytes 772
  6.5 40.9 %copy-start.1 = (f32[1,3,512]{2,0,1:T(1,128)S(1)}, f32[1,3,512]{2,0,1:T(1,128)}, u32[]{:S(2)}) copy-start(f32[1,3,512]{2,0,1:T(1,128)} %param.14) | copy-start | bytes 18436
  7.6 41.4 %copy-start.5 = (bf16[1,3,512,512]{3,2,1,0:T(8,128)(2,1)S(1)}, bf16[1,3,512,512]{3,2,1,0:T(8,128)(2,1)}, u32[]{:S(2)}) copy-start(bf16[1,3,512,512]{3,2,1,0:T(8,128)(2,1)} %param.13) | copy-start | bytes 4718596
  8.3 13.1 %all-to-all-start = ((bf16[64,8,128]{2,0,1:T(8,128)(2,1)}), bf16[64,8,128]{2,0,1:T(8,128)(2,1)S(1)}, u32[]{:S(2)}, u32[]{:S(2)}) async-start(bf16[64,8,128]{2,0,1:T(8,128)(2,1)} %copy.34), calls=%async_computation | async-start | bytes 262144 | tf_op jit(solution)/shard_map/all_to_all | solution.py:58
  14.6 56.0 %all-gather.4.cloned.1.call-start = ((), (), s32[]{:S(2)}) async-start(), calls=%async_computation.4 | async-start | bytes 1179648 | tf_op jit(solution)/shard_map/all_gather | solution.py:62
  21.4 26.6 %all-to-all-start.1 = ((bf16[64,8,128]{2,0,1:T(8,128)(2,1)}), bf16[64,8,128]{2,0,1:T(8,128)(2,1)S(1)}, u32[]{:S(2)}, u32[]{:S(2)}) async-start(bf16[64,8,128]{2,0,1:T(8,128)(2,1)} %copy.41), calls=%async_computation.1 | async-start | bytes 262144 | tf_op jit(solution)/shard_map/all_to_all | solution.py:58
  24.8 70.0 %reduce-scatter.7.cloned.1.call-start = ((), (), s32[]{:S(2)}) async-start(), calls=%async_computation.5 | async-start | bytes 81920
  50.0 1.3 %copy-start.2 = (f32[1,128]{1,0:T(1,128)S(1)}, f32[1,128]{1,0:T(1,128)}, u32[]{:S(2)}) copy-start(f32[1,128]{1,0:T(1,128)} %param.16) | copy-start | bytes 1540
  70.6 2.7 %copy-start.6 = (bf16[1024,512]{1,0:T(8,128)(2,1)S(1)}, bf16[1024,512]{1,0:T(8,128)(2,1)}, u32[]{:S(2)}) copy-start(bf16[1024,512]{1,0:T(8,128)(2,1)} %all-gather.4.cloned.1.call-done) | copy-start | bytes 3145732
  73.3 48.3 %reduce-scatter.9.cloned.1.call-start = ((), (), s32[]{:S(2)}) async-start(), calls=%async_computation.6 | async-start | bytes 81920
Sparse Core Ops, SparseCore 0:
  17.1 25.6 all-gather.3
  73.4 21.3 reduce-scatter.6
  97.5 24.0 reduce-scatter.8
where the time goes:
time: 130 us; the launch traced here: 129 us
  waiting for transfers between devices  51.5 us (40%)
  blocking collectives  39.5 us (30%)
  between operations  13.4 us (10%)
  starting transfers between devices  9.84 us (8%)
  local copies, waits for them, and re-layouts  7.22 us (6%)
  matrix products  6.64 us (5%)
  other arithmetic  1.44 us (1%)
    unnamed x5, waiting for transfers between devices  46.8 us
    all_gather x2, blocking collectives, on_device(): all_towers = lax.all_gather(compressed, 'tower', axis=0, tiled=True)  16.9 us
    all_gather x1, blocking collectives, on_device(): lax.all_gather(mlp_bias, 'rank', axis=0, tiled=True)  12.2 us
    all_gather x1, blocking collectives, on_device(): lax.all_gather(out_weight, 'rank', axis=0, tiled=True)  10.3 us
    all_to_all x2, starting transfers between devices, on_device(): lax.all_to_all(pooled[batch], 'rank', split_axis=1, concat_axis=0, tiled=...  9.72 us
    all_to_all x2, waiting for transfers between devices, on_device(): lax.all_to_all(pooled[batch], 'rank', split_axis=1, concat_axis=0, tiled=...  4.63 us
    unnamed x23, local copies, waits for them, and re-layouts  4.19 us
  transfers between devices with their start and end apart: 5, of which 3 were waited for; matrix products, arithmetic and copies ran while one was open for 7% of the time, Pallas kernels for 0%

commit v1 on v0

--- a/solution.py
+++ b/solution.py
@@ -1,13 +1,356 @@
+import functools
+
 import jax
 import jax.numpy as jnp
 from jax import lax
+from jax.experimental import pallas as pl
+from jax.experimental.pallas import tpu as pltpu
 from jax.sharding import PartitionSpec as P
 
 E = 128
 CD = 128
-
+CORES = 2
 
 epsilon = 1e-06
+MESH = pl.DeviceIdType.MESH
+
+
+def parent(source, target, chips):
+    if target == 0 and source > 1:
+        return 1
+    if target == chips - 1 and source < chips - 2:
+        return chips - 2
+    return source
+
+
+def fused(
+    n_tower,
+    n_rank,
+    order,
+    pooled,
+    cross_w,
+    cross_b,
+    compress,
+    gain,
+    mlp_w,
+    small,
+    out,
+    arrived,
+    weights,
+    compress_v,
+    bias_v,
+    gain_v,
+    bias_c,
+    gain_c,
+    first,
+    state_a,
+    state_b,
+    towers,
+    mixed,
+    rows,
+    packs,
+    hid_c,
+    parts,
+    load_sem,
+    a2a_send,
+    a2a_recv,
+    row_send,
+    row_recv,
+    mate_send,
+    mate_recv,
+    pack_send,
+    pack_recv,
+    tower_send,
+    tower_recv,
+    part_send,
+    part_recv,
+):
+    micro = pooled.shape[0]
+    block = arrived.shape[-1]
+    layers, td = cross_w.shape[1], cross_w.shape[2]
+    chips = n_rank // CORES
+    t = lax.axis_index("tower")
+    r = lax.axis_index("rank")
+    z = r // CORES
+    c = lax.rem(r, CORES)
+    mate = z * CORES + (1 - c)
+
+    loads = [
+        pltpu.make_async_copy(
+            pooled.at[:, :, pl.ds(pl.multiple_of(r * block, block), block)], arrived.at[r], load_sem.at[0]
+        ),
+        pltpu.make_async_copy(cross_b.at[0], bias_v.at[pl.ds(0, layers)], load_sem.at[1]),
+        pltpu.make_async_copy(gain, gain_v.at[pl.ds(0, 1)], load_sem.at[2]),
+        pltpu.make_async_copy(small, packs.at[r], load_sem.at[3]),
+        pltpu.make_async_copy(compress.at[0], compress_v, load_sem.at[4]),
+        pltpu.make_async_copy(mlp_w, rows.at[r], load_sem.at[5]),
+    ]
+    w_loads = [pltpu.make_async_copy(cross_w.at[0, l], weights.at[l], load_sem.at[6 + l]) for l in range(layers)]
+
+    barrier = pltpu.get_barrier_semaphore()
+    for d in range(1, n_rank):
+        pl.semaphore_signal(barrier, inc=1, device_id={"rank": lax.rem(r + d, n_rank)}, device_id_type=MESH)
+    for d in range(1, n_tower):
+        pl.semaphore_signal(barrier, inc=1, device_id={"tower": lax.rem(t + d, n_tower)}, device_id_type=MESH)
+    for copy in loads + w_loads:
+        copy.start()
+    pl.semaphore_wait(barrier, n_rank + n_tower - 2)
+
+    a2a = []
+    for b in range(micro):
+        for d in range(1, n_rank):
+            peer = lax.rem(r + d, n_rank)
+            copy = pltpu.make_async_remote_copy(
+                src_ref=pooled.at[b, :, pl.ds(pl.multiple_of(peer * block, block), block)],
+                dst_ref=arrived.at[r, b],
+                send_sem=a2a_send.at[b, d - 1],
+                recv_sem=a2a_recv.at[b, d - 1],
+                device_id={"rank": peer},
+                device_id_type=MESH,
+            )
+            copy.start()
+            a2a.append(copy)
+
+    def row_copy(source, target, src_ref):
+        return pltpu.make_async_remote_copy(
+            src_ref=src_ref,
+            dst_ref=rows.at[source * CORES + c],
+            send_sem=row_send.at[source, target],
+            recv_sem=row_recv.at[source],
+            device_id={"rank": target * CORES + c},
+            device_id_type=MESH,
+        )
+
+    def mate_copy(source, src_ref):
+        return pltpu.make_async_remote_copy(
+            src_ref=src_ref,
+            dst_ref=rows.at[source * CORES + c],
+            send_sem=mate_send.at[source],
+            recv_sem=mate_recv.at[source],
+            device_id={"rank": mate},
+            device_id_type=MESH,
+        )
+
+    packing = []
+    for d in range(1, n_rank):
+        copy = pltpu.make_async_remote_copy(
+            src_ref=small,
+            dst_ref=packs.at[r],
+            send_sem=pack_send.at[d - 1],
+            recv_sem=pack_recv.at[d - 1],
+            device_id={"rank": lax.rem(r + d, n_rank)},
+            device_id_type=MESH,
+        )
+        copy.start()
+        packing.append(copy)
+
+    for here in range(chips):
+
+        @pl.when(z == here)
+        def _():
+            for target in sorted(range(chips), key=lambda q: abs(q - here)):
+                if target != here and parent(here, target, chips) == here:
+                    row_copy(here, target, mlp_w).start()
+            mate_copy(here, mlp_w).start()
+
+    def pass_on(near):
+        for here in range(chips):
+
+            @pl.when(z == here)
+            def _():
+                for source in sorted(range(chips), key=lambda q: abs(q - here)):
+                    if source == here or (abs(source - here) == 1) != near:
+                        continue
+                    held = rows.at[source * CORES + c]
+                    row_copy(source, here, held).wait_recv()
+                    for target in range(chips):
+                        if target not in (here, source) and parent(source, target, chips) == here:
+                            row_copy(source, target, held).start()
+                    mate_copy(source, held).start()
+
+    for copy in loads:
+        copy.wait()
+    bias_c[...] = bias_v[...].T
+    gain_c[...] = gain_v[...].T
+
+    for copy in a2a:
+        copy.wait_recv()
+    per_feature = n_rank // order.shape[1]
+    height = arrived.shape[2]
+    for slot in range(order.shape[1]):
+        feature = order[0, slot]
+        for h in range(per_feature):
+            for b in range(micro):
+                first[
+                    slot * E + h * height : slot * E + (h + 1) * height, b * block : (b + 1) * block
+                ] = arrived[feature * per_feature + h, b]
+
+    current, spare = first, state_a
+    for l in range(layers):
+        w_loads[l].wait()
+        for m in range(0, td, E):
+            here = slice(m, m + E)
+            product = (
+                jnp.dot(weights[l, here, :], current[...], preferred_element_type=jnp.float32)
+                + bias_c[here, l : l + 1]
+            )
+            spare[here, :] = (
+                first[here, :].astype(jnp.float32) * product + current[here, :].astype(jnp.float32)
+            ).astype(jnp.bfloat16)
+        current, spare = spare, (state_b if spare is state_a else state_a)
+    squeezed = jnp.dot(compress_v[...], current[...], preferred_element_type=jnp.float32)
+    inverse_rms = lax.rsqrt(jnp.mean(squeezed * squeezed, axis=0, keepdims=True) + epsilon)
+    towers[t] = (squeezed * inverse_rms * gain_c[:, 0:1]).astype(jnp.bfloat16)
+
+    exchange = []
+    for d in range(1, n_tower):
+        copy = pltpu.make_async_remote_copy(
+            src_ref=towers.at[t],
+            dst_ref=towers.at[t],
+            send_sem=tower_send.at[d - 1],
+            recv_sem=tower_recv.at[d - 1],
+            device_id={"tower": lax.rem(t + d, n_tower)},
+            device_id_type=MESH,
+        )
+        copy.start()
+        exchange.append(copy)
+
+    pass_on(True)
+    for copy in packing:
+        copy.wait_recv()
+    turned_b = packs[:, 0, :].T
+    turned_o = packs[:, 1, :].T
+    for s in range(n_rank):
+        hid_c[s, 0] = turned_b[:, s : s + 1]
+        hid_c[s, 1] = turned_o[:, s : s + 1]
+
+    for copy in exchange:
+        copy.wait_recv()
+
+    values = [towers[u].astype(jnp.float32) for u in range(n_tower)]
+    gram = {}
+    for u in range(n_tower):
+        for v in range(u, n_tower):
+            gram[u, v] = gram[v, u] = jnp.sum(values[u] * values[v], axis=0, keepdims=True) / CD
+    for u in range(n_tower):
+        total = values[u]
+        for v in range(n_tower):
+            total = total + gram[u, v] * values[v]
+        mixed[u * CD : (u + 1) * CD, :] = total.astype(jnp.bfloat16)
+
+    pass_on(False)
+    side = 1 - 2 * (z // ((chips + 1) // 2))
+    score = jnp.zeros((rows.shape[1], mixed.shape[1]), jnp.float32)
+    for k in range(chips):
+        source = lax.rem(z + side * k + chips, chips)
+        for twin in range(CORES):
+            s = source * CORES + (c if twin == 0 else 1 - c)
+            if twin == 1:
+                pltpu.make_async_remote_copy(
+                    src_ref=rows.at[s],
+                    dst_ref=rows.at[s],
+                    send_sem=mate_send.at[source],
+                    recv_sem=mate_recv.at[source],
+                    device_id={"rank": mate},
+                    device_id_type=MESH,
+                ).wait_recv()
+            hidden = jnp.dot(rows[s], mixed[...], preferred_element_type=jnp.float32) + hid_c[s, 0]
+            score = score + jnp.maximum(hidden, 0.0) * hid_c[s, 1]
+    parts[t] = jnp.sum(score, axis=0, keepdims=True)
+
+    sums = []
+    for d in range(1, n_tower):
+        copy = pltpu.make_async_remote_copy(
+            src_ref=parts.at[t],
+            dst_ref=parts.at[t],
+            send_sem=part_send.at[d - 1],
+            recv_sem=part_recv.at[d - 1],
+            device_id={"tower": lax.rem(t + d, n_tower)},
+            device_id_type=MESH,
+        )
+        copy.start()
+        sums.append(copy)
+
+    for copy in a2a + packing + exchange:
+        copy.wait_send()
+    for here in range(chips):
+
+        @pl.when(z == here)
+        def _():
+            for source in range(chips):
+                for target in range(chips):
+                    if target not in (here, source) and parent(source, target, chips) == here:
+                        row_copy(source, target, rows.at[source * CORES + c]).wait_send()
+                mate_copy(source, rows.at[source * CORES + c]).wait_send()
+
+    for copy in sums:
+        copy.wait_recv()
+    logits = parts[0]
+    for u in range(1, n_tower):
+        logits = logits + parts[u]
+    width = block // n_tower
+    for u in range(n_tower):
+
+        @pl.when(t == u)
+        def _():
+            for b in range(micro):
+                out[b] = logits[:, b * block + u * width : b * block + (u + 1) * width]
+
+    for copy in sums:
+        copy.wait_send()
+
+
+def in_one_kernel(
+    n_tower, n_rank, pooled, order, cross_w, cross_b, compress, gain, mlp_w, mlp_bias, out_weight
+):
+    micro, height, samples = pooled.shape
+    block = samples // n_rank
+    _, layers, td, _ = cross_w.shape
+    hid, width = mlp_w.shape
+    chips = n_rank // CORES
+    every = micro * block
+    small = jnp.stack([mlp_bias, out_weight]).astype(jnp.float32)
+    bf16, f32 = jnp.bfloat16, jnp.float32
+    dma = pltpu.SemaphoreType.DMA
+    hbm = pl.BlockSpec(memory_space=pl.ANY)
+    return pl.pallas_call(
+        functools.partial(fused, n_tower, n_rank),
+        out_shape=jax.ShapeDtypeStruct((micro, 1, block // n_tower), f32),
+        in_specs=[pl.BlockSpec(memory_space=pltpu.SMEM)] + [hbm] * 7,
+        out_specs=pl.BlockSpec(memory_space=pltpu.VMEM),
+        scratch_shapes=[
+            pltpu.VMEM((n_rank, micro, height, block), bf16),
+            pltpu.VMEM((layers, td, td), bf16),
+            pltpu.VMEM((CD, td), bf16),
+            pltpu.VMEM((8, td), f32),
+            pltpu.VMEM((8, CD), f32),
+            pltpu.VMEM((td, 8), f32),
+            pltpu.VMEM((CD, 8), f32),
+            pltpu.VMEM((td, every), bf16),
+            pltpu.VMEM((td, every), bf16),
+            pltpu.VMEM((td, every), bf16),
+            pltpu.VMEM((n_tower, CD, every), bf16),
+            pltpu.VMEM((width, every), bf16),
+            pltpu.VMEM((n_rank, hid, width), bf16),
+            pltpu.VMEM((n_rank, 2, hid), f32),
+            pltpu.VMEM((n_rank, 2, hid, 1), f32),
+            pltpu.VMEM((n_tower, 1, every), f32),
+            dma((6 + layers,)),
+            dma((micro, n_rank - 1)),
+            dma((micro, n_rank - 1)),
+            dma((chips, chips)),
+            dma((chips,)),
+            dma((chips,)),
+            dma((chips,)),
+            dma((n_rank - 1,)),
+            dma((n_rank - 1,)),
+            dma((n_tower - 1,)),
+            dma((n_tower - 1,)),
+            dma((n_tower - 1,)),
+            dma((n_tower - 1,)),
+        ],
+        compiler_params=pltpu.CompilerParams(collective_id=0, has_side_effects=True),
+    )(order, pooled, cross_w, cross_b, compress, gain, mlp_w, small)
 
 
 def tower_block(first, weights, biases, compress, gain):
@@ -42,7 +385,7 @@
     )
 
 
-def on_device(
+def by_collectives(
     pooled,
     feature_order,
     cross_weight,
@@ -80,7 +423,17 @@
     return jnp.stack(results)
 
 
+def fits(mesh, pooled, mlp_w):
+    height, hid = pooled.shape[1], mlp_w.shape[0]
+    return mesh.shape["rank"] % CORES == 0 and E % height == 0 and height % 16 == 0 and hid % 128 == 0
+
+
 def solution(mesh):
+    def on_device(*args):
+        if fits(mesh, args[0], args[6]):
+            return in_one_kernel(mesh.shape["tower"], mesh.shape["rank"], *args)
+        return by_collectives(*args)
+
     return jax.shard_map(
         on_device,
         mesh=mesh,

time: 130 us -> 36.5 us (0.28)
  waiting for transfers between devices: 51.5 us -> 0 us
  blocking collectives: 39.5 us -> 0 us
  Pallas kernels: 0 us -> 32.5 us
  between operations: 13.4 us -> 0.01 us
  starting transfers between devices: 9.84 us -> 0 us
  matrix products: 6.64 us -> 0 us
  local copies, waits for them, and re-layouts: 7.22 us -> 2.51 us
    unnamed x5 -> x0, waiting for transfers between devices: 46.8 us -> none
    all_gather x4 -> x0, blocking collectives: 39.5 us -> none  [the longest x2 16.9 us: on_device(): all_towers = lax.all_gather(compressed, 'tower', axis=0, tiled=True)]
    pallas_call x0 -> x1, Pallas kernels: none -> 32.5 us  [in_one_kernel(): pl.pallas_call(functools.partial(fused, n_tower, n_rank), out_shape=jax.S...]
    all_to_all x2 -> x0, starting transfers between devices: 9.72 us -> none  [on_device(): lax.all_to_all(pooled[batch], 'rank', split_axis=1, concat_axis=0, tiled=...]
    dot_general x12 -> x0, matrix products: 6.64 us -> none  [the longest x2 2.44 us: logit_terms(): jnp.dot(hidden_rows, features, preferred_element_type=jnp.float32)]
    all_to_all x2 -> x0, waiting for transfers between devices: 4.63 us -> none  [on_device(): lax.all_to_all(pooled[batch], 'rank', split_axis=1, concat_axis=0, tiled=...]
    unnamed x23 -> x2, local copies, waits for them, and re-layouts: 4.19 us -> 2.51 us
    all_to_all x2 -> x0, local copies, waits for them, and re-layouts: 1.37 us -> none  [on_device(): lax.all_to_all(pooled[batch], 'rank', split_axis=1, concat_axis=0, tiled=...]
  transfers between devices with their start and end apart: 5 -> 0, of which waited for: 3 -> 0; matrix products, arithmetic and copies ran while one was open for 7% -> 0% of each run, Pallas kernels for 0% -> 0%
where the time goes in v1:
time: 36.5 us; the launch traced here: 36.3 us
  Pallas kernels  32.5 us (89%)
  local copies, waits for them, and re-layouts  2.51 us (7%)
  other arithmetic  1.24 us (3%)
    pallas_call x1, Pallas kernels, in_one_kernel(): pl.pallas_call(functools.partial(fused, n_tower, n_rank), out_shape=jax.S...  32.5 us
    unnamed x2, local copies, waits for them, and re-layouts  2.51 us
    convert_element_type x1, other arithmetic, in_one_kernel(): small = jnp.stack([mlp_bias, out_weight]).astype(jnp.float32)  1.24 us

profile of v1, /device:TPU:0, one launch (start us, length us, event | category | flops | bytes accessed | tf_op | source)
XLA Modules:
  0.0 36.3 jit_solution(18286902360715200293)
XLA Ops:
  0.0 1.2 %maximum_convert_fusion.small = f32[2,128]{1,0:T(2,128)} fusion(bf16[1,128]{1,0:T(2,128)(2,1)} %bitcast.2, bf16[1,128]{1,0:T(2,128)(2,1)} %bitcast.3), kind=kLoop, calls=%fused_computation | loop fusion | flops 1024 | bytes 1536 | tf_op jit(solution)/shard_map/convert_element_type | solution.py:312
  1.2 1.3 %copy.10.cross_b = f32[1,3,512]{2,1,0:T(4,128)} copy(f32[1,3,512]{2,0,1:T(1,128)} %param.12) | data formatting | bytes 12288 | tf_op args[3]
  2.5 32.5 %shard_map.91 = f32[2,1,32]{2,1,0:T(1,128)} custom-call(s32[1,4]{1,0:T(1,128)} %order.1, bf16[2,64,1024]{2,1,0:T(8,128)(2,1)} %pooled.1, bf16[1,3,512,512]{3,2,1,0:T(8,128)(2,1)} %cross_w.1, f32[1,3,512]{2,1,0:T(4,128)} %copy.10.cross_b, bf16[1,128,512]{2,1,0:T(8,128)(2,1)} %compress.1, f32[1,128]{1,0:T(1,128)} %gain.1, bf16[128,512]{1,0:T(8,128)(2,1)} %mlp_w.1, ...), custom_call_target="tpu_custom_call" | custom-call | tf_op jit(solution)/shard_map/pallas_call | solution.py:316
  35.0 1.2 %copy.12 = f32[2,1,32]{2,1,0:T(1,128)} copy(f32[2,1,32]{2,1,0:T(1,128)} %shard_map.91) | data formatting | bytes 512

commit v2 on v1

--- a/solution.py
+++ b/solution.py
@@ -13,14 +13,6 @@
 
 epsilon = 1e-06
 MESH = pl.DeviceIdType.MESH
-
-
-def parent(source, target, chips):
-    if target == 0 and source > 1:
-        return 1
-    if target == chips - 1 and source < chips - 2:
-        return chips - 2
-    return source
 
 
 def fused(
@@ -33,12 +25,14 @@
     compress,
     gain,
     mlp_w,
-    small,
+    hid_b,
+    hid_o,
     out,
     arrived,
     weights,
     compress_v,
     bias_v,
+    flat_v,
     gain_v,
     bias_c,
     gain_c,
@@ -48,7 +42,10 @@
     towers,
     mixed,
     rows,
-    packs,
+    packs_b,
+    packs_o,
+    flat_b,
+    flat_o,
     hid_c,
     parts,
     load_sem,
@@ -68,6 +65,7 @@
     micro = pooled.shape[0]
     block = arrived.shape[-1]
     layers, td = cross_w.shape[1], cross_w.shape[2]
+    smalls = ((hid_b, packs_b), (hid_o, packs_o))
     chips = n_rank // CORES
     t = lax.axis_index("tower")
     r = lax.axis_index("rank")
@@ -79,13 +77,14 @@
         pltpu.make_async_copy(
             pooled.at[:, :, pl.ds(pl.multiple_of(r * block, block), block)], arrived.at[r], load_sem.at[0]
         ),
-        pltpu.make_async_copy(cross_b.at[0], bias_v.at[pl.ds(0, layers)], load_sem.at[1]),
-        pltpu.make_async_copy(gain, gain_v.at[pl.ds(0, 1)], load_sem.at[2]),
-        pltpu.make_async_copy(small, packs.at[r], load_sem.at[3]),
-        pltpu.make_async_copy(compress.at[0], compress_v, load_sem.at[4]),
-        pltpu.make_async_copy(mlp_w, rows.at[r], load_sem.at[5]),
+        pltpu.make_async_copy(cross_b, bias_v, load_sem.at[1]),
+        pltpu.make_async_copy(gain, gain_v, load_sem.at[2]),
+        pltpu.make_async_copy(hid_b, packs_b.at[r], load_sem.at[3]),
+        pltpu.make_async_copy(hid_o, packs_o.at[r], load_sem.at[4]),
+        pltpu.make_async_copy(compress.at[0], compress_v, load_sem.at[5]),
+        pltpu.make_async_copy(mlp_w, rows.at[r], load_sem.at[6]),
     ]
-    w_loads = [pltpu.make_async_copy(cross_w.at[0, l], weights.at[l], load_sem.at[6 + l]) for l in range(layers)]
+    w_loads = [pltpu.make_async_copy(cross_w.at[0, l], weights.at[l], load_sem.at[7 + l]) for l in range(layers)]
 
     barrier = pltpu.get_barrier_semaphore()
     for d in range(1, n_rank):
@@ -96,85 +95,113 @@
         copy.start()
     pl.semaphore_wait(barrier, n_rank + n_tower - 2)
 
+    def spread(b, source, target, src_ref):
+        return pltpu.make_async_remote_copy(
+            src_ref=src_ref,
+            dst_ref=arrived.at[source, b],
+            send_sem=a2a_send.at[b, target],
+            recv_sem=a2a_recv.at[b, source],
+            device_id={"rank": target},
+            device_id_type=MESH,
+        )
+
+    def chip_at(k):
+        return lax.rem(z + k + chips, chips)
+
+    others = [
+        chip_at(k) * CORES + (c if twin == 0 else 1 - c)
+        for k in sorted(range(chips), key=lambda k: -min(k, chips - k))
+        for twin in range(CORES)
+        if (k, twin) != (0, 0)
+    ]
     a2a = []
     for b in range(micro):
-        for d in range(1, n_rank):
-            peer = lax.rem(r + d, n_rank)
+        for peer in others:
+            columns = pl.ds(pl.multiple_of(peer * block, block), block)
+            copy = spread(b, r, peer, pooled.at[b, :, columns])
+            copy.start()
+            a2a.append(copy)
+
+    half = rows.shape[1] // 2
+    seen = set()
+
+    def piece(k, h):
+        return rows.at[chip_at(k) * CORES + c, pl.ds(h * half, half)]
+
+    def row_copy(k, h, way, src_ref):
+        return pltpu.make_async_remote_copy(
+            src_ref=src_ref,
+            dst_ref=piece(k, h),
+            send_sem=row_send.at[abs(k), h, max(way, 0)],
+            recv_sem=row_recv.at[chip_at(k), h],
+            device_id={"rank": chip_at(way) * CORES + c},
+            device_id_type=MESH,
+        )
+
+    def arrive(k, h):
+        if k % chips and (k % chips, h) not in seen:
+            seen.add((k % chips, h))
+            row_copy(k, h, 1, piece(k, h)).wait_recv()
+
+    row_sends = []
+
+    def hop(s):
+        for h, way in ((0, 1), (1, -1), (1, 1), (0, -1)):
+            reach = chips // 2 if (h, way) in ((0, 1), (1, -1)) else (chips - 1) // 2
+            if s < reach:
+                k = -way * s
+                if s:
+                    arrive(k, h)
+                copy = row_copy(k, h, way, piece(k, h) if s else mlp_w.at[pl.ds(h * half, half)])
+                copy.start()
+                row_sends.append(copy)
+
+    def mate_copy(k, src_ref):
+        return pltpu.make_async_remote_copy(
+            src_ref=src_ref,
+            dst_ref=rows.at[chip_at(k) * CORES + c],
+            send_sem=mate_send.at[k],
+            recv_sem=mate_recv.at[k],
+            device_id={"rank": mate},
+            device_id_type=MESH,
+        )
+
+    def share(k):
+        for h in range(2):
+            arrive(k, h)
+        copy = mate_copy(k, rows.at[chip_at(k) * CORES + c] if k else mlp_w)
+        copy.start()
+        row_sends.append(copy)
+
+    packing = []
+    for d in range(1, n_rank):
+        for i, (source, target) in enumerate(smalls):
             copy = pltpu.make_async_remote_copy(
-                src_ref=pooled.at[b, :, pl.ds(pl.multiple_of(peer * block, block), block)],
-                dst_ref=arrived.at[r, b],
-                send_sem=a2a_send.at[b, d - 1],
-                recv_sem=a2a_recv.at[b, d - 1],
-                device_id={"rank": peer},
+                src_ref=source,
+                dst_ref=target.at[r],
+                send_sem=pack_send.at[i, d - 1],
+                recv_sem=pack_recv.at[i, d - 1],
+                device_id={"rank": lax.rem(r + d, n_rank)},
                 device_id_type=MESH,
             )
             copy.start()
-            a2a.append(copy)
-
-    def row_copy(source, target, src_ref):
-        return pltpu.make_async_remote_copy(
-            src_ref=src_ref,
-            dst_ref=rows.at[source * CORES + c],
-            send_sem=row_send.at[source, target],
-            recv_sem=row_recv.at[source],
-            device_id={"rank": target * CORES + c},
-            device_id_type=MESH,
-        )
-
-    def mate_copy(source, src_ref):
-        return pltpu.make_async_remote_copy(
-            src_ref=src_ref,
-            dst_ref=rows.at[source * CORES + c],
-            send_sem=mate_send.at[source],
-            recv_sem=mate_recv.at[source],
-            device_id={"rank": mate},
-            device_id_type=MESH,
-        )
-
-    packing = []
-    for d in range(1, n_rank):
-        copy = pltpu.make_async_remote_copy(
-            src_ref=small,
-            dst_ref=packs.at[r],
-            send_sem=pack_send.at[d - 1],
-            recv_sem=pack_recv.at[d - 1],
-            device_id={"rank": lax.rem(r + d, n_rank)},
-            device_id_type=MESH,
-        )
-        copy.start()
-        packing.append(copy)
-
-    for here in range(chips):
-
-        @pl.when(z == here)
-        def _():
-            for target in sorted(range(chips), key=lambda q: abs(q - here)):
-                if target != here and parent(here, target, chips) == here:
-                    row_copy(here, target, mlp_w).start()
-            mate_copy(here, mlp_w).start()
-
-    def pass_on(near):
-        for here in range(chips):
-
-            @pl.when(z == here)
-            def _():
-                for source in sorted(range(chips), key=lambda q: abs(q - here)):
-                    if source == here or (abs(source - here) == 1) != near:
-                        continue
-                    held = rows.at[source * CORES + c]
-                    row_copy(source, here, held).wait_recv()
-                    for target in range(chips):
-                        if target not in (here, source) and parent(source, target, chips) == here:
-                            row_copy(source, target, held).start()
-                    mate_copy(source, held).start()
+            packing.append(copy)
+
+    hop(0)
+    share(0)
+    near = [k for k in range(1, chips) if min(k, chips - k) == 1]
+    far = [k for k in sorted(range(1, chips), key=lambda k: min(k, chips - k)) if k not in near]
 
     for copy in loads:
         copy.wait()
-    bias_c[...] = bias_v[...].T
-    gain_c[...] = gain_v[...].T
-
-    for copy in a2a:
-        copy.wait_recv()
+    for l in range(layers):
+        flat_v[l : l + 1, :] = bias_v[l]
+    bias_c[...] = flat_v[...].T
+    gain_c[...] = jnp.broadcast_to(gain_v[...], (8, CD)).T
+
+    for b in range(micro):
+        for peer in others:
+            spread(b, peer, r, arrived.at[peer, b]).wait_recv()
     per_feature = n_rank // order.shape[1]
     height = arrived.shape[2]
     for slot in range(order.shape[1]):
@@ -197,6 +224,8 @@
             spare[here, :] = (
                 first[here, :].astype(jnp.float32) * product + current[here, :].astype(jnp.float32)
             ).astype(jnp.bfloat16)
+        if l == layers - 1:
+            hop(1)
         current, spare = spare, (state_b if spare is state_a else state_a)
     squeezed = jnp.dot(compress_v[...], current[...], preferred_element_type=jnp.float32)
     inverse_rms = lax.rsqrt(jnp.mean(squeezed * squeezed, axis=0, keepdims=True) + epsilon)
@@ -215,11 +244,17 @@
         copy.start()
         exchange.append(copy)
 
-    pass_on(True)
+    for k in near:
+        share(k)
+    for step in range(2, chips // 2):
+        hop(step)
     for copy in packing:
         copy.wait_recv()
-    turned_b = packs[:, 0, :].T
-    turned_o = packs[:, 1, :].T
+    for s in range(n_rank):
+        flat_b[s : s + 1, :] = packs_b[s].astype(jnp.float32)
+        flat_o[s : s + 1, :] = packs_o[s].astype(jnp.float32)
+    turned_b = flat_b[...].T
+    turned_o = flat_o[...].T
     for s in range(n_rank):
         hid_c[s, 0] = turned_b[:, s : s + 1]
         hid_c[s, 1] = turned_o[:, s : s + 1]
@@ -238,24 +273,33 @@
             total = total + gram[u, v] * values[v]
         mixed[u * CD : (u + 1) * CD, :] = total.astype(jnp.bfloat16)
 
-    pass_on(False)
-    side = 1 - 2 * (z // ((chips + 1) // 2))
     score = jnp.zeros((rows.shape[1], mixed.shape[1]), jnp.float32)
-    for k in range(chips):
-        source = lax.rem(z + side * k + chips, chips)
-        for twin in range(CORES):
-            s = source * CORES + (c if twin == 0 else 1 - c)
-            if twin == 1:
-                pltpu.make_async_remote_copy(
-                    src_ref=rows.at[s],
-                    dst_ref=rows.at[s],
-                    send_sem=mate_send.at[source],
-                    recv_sem=mate_recv.at[source],
-                    device_id={"rank": mate},
-                    device_id_type=MESH,
-                ).wait_recv()
-            hidden = jnp.dot(rows[s], mixed[...], preferred_element_type=jnp.float32) + hid_c[s, 0]
-            score = score + jnp.maximum(hidden, 0.0) * hid_c[s, 1]
+
+    def add(s, score):
+        hidden = jnp.dot(rows[s], mixed[...], preferred_element_type=jnp.float32) + hid_c[s, 0]
+        return score + jnp.maximum(hidden, 0.0) * hid_c[s, 1]
+
+    def add_mate(k, score):
+        s = chip_at(k) * CORES + 1 - c
+        pltpu.make_async_remote_copy(
+            src_ref=rows.at[s],
+            dst_ref=rows.at[s],
+            send_sem=mate_send.at[k],
+            recv_sem=mate_recv.at[k],
+            device_id={"rank": mate},
+            device_id_type=MESH,
+        ).wait_recv()
+        return add(s, score)
+
+    for k in [0] + near:
+        score = add(chip_at(k) * CORES + c, score)
+    for k in [0] + near:
+        score = add_mate(k, score)
+    for k in far:
+        share(k)
+        score = add(chip_at(k) * CORES + c, score)
+    for k in far:
+        score = add_mate(k, score)
     parts[t] = jnp.sum(score, axis=0, keepdims=True)
 
     sums = []
@@ -271,18 +315,8 @@
         copy.start()
         sums.append(copy)
 
-    for copy in a2a + packing + exchange:
+    for copy in a2a + packing + exchange + row_sends:
         copy.wait_send()
-    for here in range(chips):
-
-        @pl.when(z == here)
-        def _():
-            for source in range(chips):
-                for target in range(chips):
-                    if target not in (here, source) and parent(source, target, chips) == here:
-                        row_copy(source, target, rows.at[source * CORES + c]).wait_send()
-                mate_copy(source, rows.at[source * CORES + c]).wait_send()
-
     for copy in sums:
         copy.wait_recv()
     logits = parts[0]
@@ -309,21 +343,21 @@
     hid, width = mlp_w.shape
     chips = n_rank // CORES
     every = micro * block
-    small = jnp.stack([mlp_bias, out_weight]).astype(jnp.float32)
     bf16, f32 = jnp.bfloat16, jnp.float32
     dma = pltpu.SemaphoreType.DMA
     hbm = pl.BlockSpec(memory_space=pl.ANY)
     return pl.pallas_call(
         functools.partial(fused, n_tower, n_rank),
         out_shape=jax.ShapeDtypeStruct((micro, 1, block // n_tower), f32),
-        in_specs=[pl.BlockSpec(memory_space=pltpu.SMEM)] + [hbm] * 7,
+        in_specs=[pl.BlockSpec(memory_space=pltpu.SMEM)] + [hbm] * 8,
         out_specs=pl.BlockSpec(memory_space=pltpu.VMEM),
         scratch_shapes=[
             pltpu.VMEM((n_rank, micro, height, block), bf16),
             pltpu.VMEM((layers, td, td), bf16),
             pltpu.VMEM((CD, td), bf16),
+            pltpu.VMEM((layers, 1, td), f32),
             pltpu.VMEM((8, td), f32),
-            pltpu.VMEM((8, CD), f32),
+            pltpu.VMEM((1, CD), f32),
             pltpu.VMEM((td, 8), f32),
             pltpu.VMEM((CD, 8), f32),
             pltpu.VMEM((td, every), bf16),
@@ -332,25 +366,38 @@
             pltpu.VMEM((n_tower, CD, every), bf16),
             pltpu.VMEM((width, every), bf16),
             pltpu.VMEM((n_rank, hid, width), bf16),
-            pltpu.VMEM((n_rank, 2, hid), f32),
+            pltpu.VMEM((n_rank, 1, hid), bf16),
+            pltpu.VMEM((n_rank, 1, hid), bf16),
+            pltpu.VMEM((n_rank, hid), f32),
+            pltpu.VMEM((n_rank, hid), f32),
             pltpu.VMEM((n_rank, 2, hid, 1), f32),
             pltpu.VMEM((n_tower, 1, every), f32),
-            dma((6 + layers,)),
-            dma((micro, n_rank - 1)),
-            dma((micro, n_rank - 1)),
-            dma((chips, chips)),
+            dma((7 + layers,)),
+            dma((micro, n_rank)),
+            dma((micro, n_rank)),
+            dma((chips, 2, 2)),
+            dma((chips, 2)),
             dma((chips,)),
             dma((chips,)),
-            dma((chips,)),
-            dma((n_rank - 1,)),
-            dma((n_rank - 1,)),
+            dma((2, n_rank - 1)),
+            dma((2, n_rank - 1)),
             dma((n_tower - 1,)),
             dma((n_tower - 1,)),
             dma((n_tower - 1,)),
             dma((n_tower - 1,)),
         ],
         compiler_params=pltpu.CompilerParams(collective_id=0, has_side_effects=True),
-    )(order, pooled, cross_w, cross_b, compress, gain, mlp_w, small)
+    )(
+        order,
+        pooled,
+        cross_w,
+        cross_b.swapaxes(0, 1),
+        compress,
+        gain,
+        mlp_w,
+        mlp_bias[None],
+        out_weight[None],
+    )
 
 
 def tower_block(first, weights, biases, compress, gain):

time: 36.5 us -> 30 us (0.82)
  the two profiles are of different devices: /device:TPU:0 before, /device:TPU:9 now
where the time goes in v2:
time: 30 us; the launch traced here: 29.8 us
  Pallas kernels  28.6 us (95%)
  local copies, waits for them, and re-layouts  1.24 us (4%)
    pallas_call x1, Pallas kernels, in_one_kernel(): pl.pallas_call(functools.partial(fused, n_tower, n_rank), out_shape=jax.S...  28.6 us
    unnamed x1, local copies, waits for them, and re-layouts  1.24 us

profile of v2, /device:TPU:9, one launch (start us, length us, event | category | flops | bytes accessed | tf_op | source)
XLA Modules:
  0.0 29.8 jit_solution(14716284529306438792)
XLA Ops:
  0.0 28.6 %shard_map.91 = f32[2,1,32]{2,1,0:T(1,128)} custom-call(s32[1,4]{1,0:T(1,128)} %order.1, bf16[2,64,1024]{2,1,0:T(8,128)(2,1)} %pooled.1, bf16[1,3,512,512]{3,2,1,0:T(8,128)(2,1)} %cross_w.1, f32[3,1,512]{2,1,0:T(1,128)} %bitcast.3, bf16[1,128,512]{2,1,0:T(8,128)(2,1)} %compress.1, f32[1,128]{1,0:T(1,128)} %gain.1, bf16[128,512]{1,0:T(8,128)(2,1)} %mlp_w.1, ...), custom_call_target="tpu_custom_call" | custom-call | tf_op jit(solution)/shard_map/pallas_call | solution.py:349
  28.6 1.2 %copy.11 = f32[2,1,32]{2,1,0:T(1,128)} copy(f32[2,1,32]{2,1,0:T(1,128)} %shard_map.91) | data formatting | bytes 512
